TPU v7x, 32 devices: a whole 2x2x4 slice. The times are simulated.
32 devices in a mesh: groups: 2 (over y), ulysses: 4 (over z), blk: 2 (over x), handoff: 2 (over core).
Axes of the slice: x: 2, y: 2, z: 4, core: 2. Of those that a mesh axis runs over, the one named last changes fastest.
Arguments:
- queries: bfloat16 [4, 512, 4096], P(('groups', 'handoff'), ('blk', 'ulysses')), parts along dimension 0, may hold values from -24 to 24
- keys: bfloat16 [4, 512, 2048], P(('groups', 'handoff'), ('blk', 'ulysses')), parts along dimension 0, may hold values from -7.5 to 7.5
- values: bfloat16 [4, 512, 2048], P(('groups', 'handoff'), ('blk', 'ulysses')), parts along dimension 0, may hold values from -6 to 6
- request_pages: int32 [4, 4], P('groups'), parts along dimension 0, may hold values from 1 to 4, 8 in all within a row
- page_table: int32 [4, 8], P('groups'), parts along dimension 0, may hold values from 0 to 15, as said below
Outputs:
- attended: bfloat16 [4, 512, 4096], P(('groups', 'handoff'), ('blk', 'ulysses')), parts along dimension 0
- cache_keys: bfloat16 [32, 16, 64, 128], P(('groups', 'blk', 'handoff'), 'ulysses'), parts along dimension 0
- cache_values: bfloat16 [32, 16, 64, 128], P(('groups', 'blk', 'handoff'), 'ulysses'), parts along dimension 0
There are 2 independent parts, one for each index of `groups`. A program takes and returns all parts, laid end to end along the dimension named above; each array names one. Nothing has to cross between parts.
Inputs may be any that keep to these rules, and one draw needn't show every extreme that they name: `request_pages`: A pack's 4 requests fill its 8 pages; the longest holds exactly 4 of them. `page_table`: all rows together name every pool page once; the 4 pages of each aligned run of 4 pages of a pack's row go in equal numbers to each aligned run of 4 pool pages.
All inputs are finite; a program needn't handle non-finite values.
Results may differ from a plain program's by a relative error of at most 0.012.
Values may be sent and summed in bfloat16 or wider, within the bound.
A program may use at most 64 MiB of HBM per device.

v0:
```python
import math
import jax
import jax.numpy as jnp
from jax import lax
from jax.sharding import PartitionSpec as P

QH = 32
KVH = 16
HD = 128
WINDOW = 4096
PAGE = 64
QUERY_SCALE = 144.0 ** (-0.5)
SOFT_CAP = 50.0
ROPE_BASE = 10000.0


def from_behind(block, axis, distance):
    devices = range(lax.axis_size(axis))
    route = [(i - distance, i) for i in devices if i - distance in devices]
    return lax.ppermute(block, axis, route)


def request_marks(pages_row, positions):
    request_ends = jnp.cumsum(pages_row, dtype=jnp.int32) * PAGE
    request_starts = request_ends - pages_row * PAGE
    owner_index = jnp.sum((positions[:, None] >= request_ends[None, :]).astype(jnp.int32), axis=1)
    first_token = jnp.max(
        jnp.where(positions[:, None] >= request_starts[None, :], request_starts[None, :], 0), axis=1
    )
    return (owner_index, positions - first_token)


def rotate(head_rows, offsets):
    head_width = head_rows.shape[-1]
    half_width = head_width // 2
    frequency = ROPE_BASE ** (-(2.0 * jnp.arange(half_width, dtype=jnp.float32)) / head_width)
    angles = offsets.astype(jnp.float32)[:, None] * frequency[None, :]
    cosine = jnp.cos(angles)[:, None, :]
    sines = jnp.sin(angles)[:, None, :]
    as_float = head_rows.astype(jnp.float32)
    front_half = as_float[..., :half_width]
    back_half = as_float[..., half_width:]
    turned = jnp.concatenate(
        [front_half * cosine - back_half * sines, back_half * cosine + front_half * sines], axis=-1
    )
    return turned.astype(jnp.bfloat16)


def body(queries, keys, values, request_pages, page_table):
    local_rows = queries.shape[1]
    ulysses_size = lax.axis_size("ulysses")
    blk_size = lax.axis_size("blk")
    core_count = lax.axis_size("handoff")
    pack_index = lax.axis_index("handoff")
    blk_index = lax.axis_index("blk")
    shard_rows = local_rows * ulysses_size
    window = min(WINDOW, page_table.shape[1] // 2 * PAGE)
    earlier_count = min(window // shard_rows, blk_size - 1)
    kv_local = KVH // ulysses_size
    group_size = QH // KVH
    query_split = queries[0].reshape(local_rows, ulysses_size, kv_local * group_size * HD)
    key_split = keys[0].reshape(local_rows, ulysses_size, kv_local * HD)
    value_split = values[0].reshape(local_rows, ulysses_size, kv_local * HD)
    pages_row = lax.dynamic_index_in_dim(request_pages, pack_index, 0, keepdims=False)
    positions = blk_index * shard_rows + jnp.arange(shard_rows, dtype=jnp.int32)
    query_owner, offsets = request_marks(pages_row, positions)
    queries_moved, keys_moved, values_moved = (
        lax.all_to_all(query_split, "ulysses", split_axis=1, concat_axis=0, tiled=True),
        lax.all_to_all(key_split, "ulysses", split_axis=1, concat_axis=0, tiled=True),
        lax.all_to_all(value_split, "ulysses", split_axis=1, concat_axis=0, tiled=True),
    )
    key_turned = rotate(keys_moved.reshape(shard_rows, kv_local, HD), offsets)
    local_kv = jnp.stack(
        [
            key_turned.reshape(shard_rows, kv_local * HD),
            values_moved.reshape(shard_rows, kv_local * HD),
        ]
    )
    earlier = []
    carried = local_kv
    for hop in range(earlier_count):
        carried = from_behind(carried, "blk", 1)
        earlier.append(carried)
    slots_dev = shard_rows // PAGE
    sources = blk_size * core_count
    per_peer = slots_dev // sources
    pack_row = lax.dynamic_index_in_dim(page_table, pack_index, 0, keepdims=False)
    my_pages = lax.dynamic_slice_in_dim(pack_row, blk_index * slots_dev, slots_dev)
    send_order = jnp.argsort(my_pages)
    paged = local_kv.reshape(2, slots_dev, PAGE, kv_local, HD)[:, send_order]
    paged = jnp.transpose(paged, (0, 1, 3, 2, 4))
    outgoing = paged.reshape(2, sources, per_peer, kv_local, PAGE, HD)
    received = lax.all_to_all(outgoing, ("blk", "handoff"), split_axis=1, concat_axis=1, tiled=True)
    received = received.reshape(2, slots_dev, kv_local, PAGE, HD)
    page_grid = jnp.transpose(
        page_table.reshape(core_count, blk_size, slots_dev), (1, 0, 2)
    ).reshape(sources, slots_dev)
    my_index = blk_index * core_count + pack_index
    is_here = page_grid // slots_dev == my_index
    picked = (
        jnp.sort(jnp.where(is_here, page_grid, page_table.size), axis=1)[:, :per_peer]
        - my_index * slots_dev
    )
    inverse = jnp.argsort(picked.reshape(-1))
    cache_keys = received[0][inverse]
    cache_values = received[1][inverse]
    query_turned = rotate(queries_moved.reshape(shard_rows, kv_local * group_size, HD), offsets)
    query_turned = query_turned.reshape(shard_rows, kv_local, group_size, HD)
    front_rows = window - earlier_count * shard_rows
    front_zeros = jnp.zeros((2, front_rows, kv_local * HD), jnp.bfloat16)
    table_kv = jnp.concatenate([front_zeros] + earlier[::-1] + [local_kv], axis=1)
    key_positions = (
        blk_index * shard_rows - window + jnp.arange(window + shard_rows, dtype=jnp.int32)
    )
    key_owner, unused_offsets = request_marks(pages_row, key_positions)
    block_rows = math.gcd(shard_rows, 128)
    key_span = window + block_rows

    def attend(offset):
        query_block = lax.dynamic_slice_in_dim(query_turned, offset, block_rows, 0)
        kv_block = lax.dynamic_slice_in_dim(table_kv, offset, key_span, 1)
        key_block = kv_block[0].reshape(key_span, kv_local, HD)
        value_block = kv_block[1].reshape(key_span, kv_local, HD)
        scores = (
            jnp.einsum("qgrd,kgd->gqrk", query_block, key_block, preferred_element_type=jnp.float32)
            * QUERY_SCALE
        )
        capped = SOFT_CAP * jnp.tanh(scores / SOFT_CAP)
        query_pos = lax.dynamic_slice_in_dim(positions, offset, block_rows)
        query_part = lax.dynamic_slice_in_dim(query_owner, offset, block_rows)
        key_pos = lax.dynamic_slice_in_dim(key_positions, offset, key_span)
        key_part = lax.dynamic_slice_in_dim(key_owner, offset, key_span)
        distance = query_pos[:, None] - key_pos[None, :]
        allowed = (
            (query_part[:, None] == key_part[None, :])
            & (distance >= 0)
            & (distance < window)
            & (key_pos[None, :] >= 0)
        )
        weights = jnp.where(allowed[None, :, None, :], jnp.exp(capped), jnp.float32(0.0))
        totals = jnp.sum(weights, axis=-1)
        mixture = jnp.einsum(
            "gqrk,kgd->qgrd",
            weights.astype(jnp.bfloat16),
            value_block,
            preferred_element_type=jnp.float32,
        )
        return (mixture / jnp.transpose(totals, (1, 0, 2))[..., None]).astype(jnp.bfloat16)

    starts = jnp.arange(shard_rows // block_rows, dtype=jnp.int32) * block_rows
    blocks = lax.map(attend, starts)
    outgoing_heads = blocks.reshape(ulysses_size, local_rows, 1, kv_local * group_size * HD)
    merged = lax.all_to_all(outgoing_heads, "ulysses", split_axis=0, concat_axis=2, tiled=True)
    attended = merged.reshape(1, local_rows, QH * HD)
    return (attended, cache_keys, cache_values)


def solution(mesh):
    in_specs = (
        P(("groups", "handoff"), ("blk", "ulysses"), None),
        P(("groups", "handoff"), ("blk", "ulysses"), None),
        P(("groups", "handoff"), ("blk", "ulysses"), None),
        P("groups", None),
        P("groups", None),
    )
    out_specs = (
        P(("groups", "handoff"), ("blk", "ulysses"), None),
        P(("groups", "blk", "handoff"), "ulysses", None, None),
        P(("groups", "blk", "handoff"), "ulysses", None, None),
    )
    return jax.shard_map(body, mesh=mesh, in_specs=in_specs, out_specs=out_specs, check_vma=False)
```

profile of v0, /device:TPU:0, one launch (start us, length us, event | category | flops | bytes accessed | tf_op | source)
XLA Modules:
  0.0 87.5 jit_solution(2109109784763567030)
XLA Ops:
  0.7 1.2 %reshape_squeeze.9 = bf16[64,4,512]{2,1,0:T(4,128)(2,1)S(1)} reshape(bf16[1,64,2048]{2,1,0:T(8,128)(2,1)} %param.8) | data formatting | bytes 524288 | tf_op jit(solution)/shard_map/reshape;squeeze | solution.py:62
  1.8 0.7 copy.70
  2.6 6.5 %all-to-all-start = ((bf16[64,4,512]{2,0,1:T(8,128)(2,1)}), bf16[64,4,512]{2,0,1:T(8,128)(2,1)S(1)}, u32[]{:S(2)}, u32[]{:S(2)}) async-start(bf16[64,4,512]{2,0,1:T(8,128)(2,1)} %copy.70), calls=%async_computation | async-start | bytes 524288 | tf_op jit(solution)/shard_map/all_to_all | solution.py:69
  9.1 0.2 reduce-window.4
  9.3 0.1 reshape.241
  9.5 0.7 sort.46
  10.2 0.1 copy.85
  10.3 0.2 reshape_squeeze.10
  10.5 0.7 copy.71
  11.3 0.1 convert_reduce_fusion.1
  11.4 6.6 %all-to-all-done = bf16[64,4,512]{2,0,1:T(8,128)(2,1)S(1)} async-done(((bf16[64,4,512]{2,0,1:T(8,128)(2,1)}), bf16[64,4,512]{2,0,1:T(8,128)(2,1)S(1)}, u32[]{:S(2)}, u32[]{:S(2)}) %all-to-all-start) | async-done | bytes 262176 | tf_op jit(solution)/shard_map/all_to_all | solution.py:69
  18.0 3.4 %all-to-all-start.1 = ((bf16[64,4,512]{2,0,1:T(8,128)(2,1)}), bf16[64,4,512]{2,0,1:T(8,128)(2,1)S(1)}, u32[]{:S(2)}, u32[]{:S(2)}) async-start(bf16[64,4,512]{2,0,1:T(8,128)(2,1)} %copy.71), calls=%async_computation.1 | async-start | bytes 524288 | tf_op jit(solution)/shard_map/all_to_all | solution.py:70
  21.4 0.4 reshape_squeeze.11
  21.8 1.0 %copy.72 = bf16[64,4,1024]{2,0,1:T(8,128)(2,1)} copy(bf16[64,4,1024]{2,1,0:T(4,128)(2,1)S(1)} %reshape_squeeze.11) | data formatting | bytes 1048576 | tf_op jit(solution)/shard_map/reshape;squeeze | solution.py:61
  22.8 0.6 sort.47
  23.4 0.1 convert_reduce_fusion
  23.5 0.5 multiply_cosine_fusion
  24.0 4.4 %all-to-all-done.1 = bf16[64,4,512]{2,0,1:T(8,128)(2,1)S(1)} async-done(((bf16[64,4,512]{2,0,1:T(8,128)(2,1)}), bf16[64,4,512]{2,0,1:T(8,128)(2,1)S(1)}, u32[]{:S(2)}, u32[]{:S(2)}) %all-to-all-start.1) | async-done | bytes 262176 | tf_op jit(solution)/shard_map/all_to_all | solution.py:70
  28.4 3.5 %all-to-all-start.2 = ((bf16[64,4,1024]{2,0,1:T(8,128)(2,1)}), bf16[64,4,1024]{2,0,1:T(8,128)(2,1)S(1)}, u32[]{:S(2)}, u32[]{:S(2)}) async-start(bf16[64,4,1024]{2,0,1:T(8,128)(2,1)} %copy.72), calls=%async_computation.2 | async-start | bytes 1048576 | tf_op jit(solution)/shard_map/all_to_all | solution.py:68
  31.9 0.2 reshape.244
  32.1 0.5 multiply_subtract_fusion
  32.6 0.4 maximum_convert_fusion
  33.0 0.1 convert_element_type.81
  33.3 4.2 %collective-permute-start = (bf16[2,256,512]{2,1,0:T(8,128)(2,1)S(1)}, bf16[2,256,512]{2,1,0:T(8,128)(2,1)}, u32[]{:S(2)}, u32[]{:S(2)}) collective-permute-start(bf16[2,256,512]{2,1,0:T(8,128)(2,1)S(1)} %pad_maximum_fusion), channel_id=1, source_target_pairs={{0,2},{1,3},{4,6},{5,7},{8,10},{9,11},{12,14},{13,15},{16,18},{17,... | collective-permute-start | bytes 1572872 | tf_op jit(solution)/shard_map/ppermute | solution.py:20
  37.6 1.4 %gather_fusion = bf16[4,2,64,4,128]{4,2,3,1,0:T(8,128)(2,1)} fusion(bf16[2,4,64,4,128]{4,2,3,1,0:T(8,128)(2,1)S(1)} %pad_maximum_fusion.2, s32[1024]{0:T(1024)S(1)} %pad_clamp_fusion.1), kind=kCustom, calls=%fused_computation | custom fusion | bytes 1048592 | tf_op jit(solution)/shard_map/gather | solution.py:90
  39.0 4.6 %all-to-all-done.2 = bf16[64,4,1024]{2,0,1:T(8,128)(2,1)S(1)} async-done(((bf16[64,4,1024]{2,0,1:T(8,128)(2,1)}), bf16[64,4,1024]{2,0,1:T(8,128)(2,1)S(1)}, u32[]{:S(2)}, u32[]{:S(2)}) %all-to-all-start.2) | async-done | bytes 524320 | tf_op jit(solution)/shard_map/all_to_all | solution.py:68
  43.6 3.5 %all-to-all-start.4 = ((bf16[2,4,1,4,64,128]{5,4,3,0,2,1:T(8,128)(2,1)}), bf16[2,4,1,4,64,128]{5,4,3,0,2,1:T(8,128)(2,1)S(1)}, u32[]{:S(2)}, u32[]{:S(2)}) async-start(bf16[2,4,1,4,64,128]{5,4,3,0,2,1:T(8,128)(2,1)} %bitcast.30), calls=%async_computation.4 | async-start | bytes 1048576 | tf_op jit(solution)/shard_map/all_to_all | solution.py:93
  47.1 0.1 bitcast_convert_fusion
  47.2 0.2 copy.104
  47.4 0.5 subtract_convert_fusion
  48.1 0.3 pad_maximum_fusion.1
  48.4 1.1 %maximum_maximum_fusion = bf16[2,512,512]{2,1,0:T(8,128)(2,1)S(1)} fusion(bf16[1,256,512]{2,1,0:T(8,128)(2,1)S(1)} %bitcast.114, bf16[1,256,512]{2,1,0:T(8,128)(2,1)S(1)} %convert_element_type.81, bf16[2,256,512]{2,1,0:T(8,128)(2,1)} %collective-permute-done), kind=kLoop, calls=%fused_computation.20 | loop fusion | flops 3145728 | bytes 2097152 | tf_op jit(solution)/shard_map/concatenate | solution.py:111
  49.5 15.4 %while.12 = (s32[]{:T(128)}, bf16[2,128,4,2,128]{4,3,2,1,0:T(2,128)(2,1)}, s32[2]{0:T(128)S(1)}, bf16[2,512,512]{2,1,0:T(8,128)(2,1)S(1)}, s32[256]{0:T(256)S(1)...) while((s32[]{:T(128)}, ...), condition=%wide.region_6.7_spmd, body=%wide.region_4.6_spmd.sunk | while | flops 203898240 | bytes 11392056 | solution.py:151
  49.5 0.6 dynamic_slice.76
  53.3 0.1 dynamic_slice.77
  53.6 0.1 fusion.28
  53.8 0.2 constant_dynamic-slice_fusion.4
  54.0 0.2 copy.108
  54.2 0.2 copy.109
  54.4 0.7 fusion.29
  55.1 0.4 fusion.30
  55.5 0.2 copy.110
  55.7 0.5 copy-done.1
  56.2 0.2 constant_dynamic-update-slice_fusion.2
  56.4 0.8 copy-done.2
  57.2 0.6 dynamic_slice.76
  61.3 0.1 fusion.28
  61.4 0.2 constant_dynamic-slice_fusion.4
  61.6 0.2 copy.108
  61.9 0.2 copy.109
  62.1 0.7 fusion.29
  62.8 0.4 fusion.30
  63.2 0.2 copy.110
  63.4 0.5 copy-done.1
  63.9 0.2 constant_dynamic-update-slice_fusion.2
  64.1 0.8 copy-done.2
  64.9 2.2 %reshape.238 = bf16[4,64,1,1024]{3,1,0,2:T(8,128)(2,1)} reshape(bf16[2,128,4,2,128]{4,3,2,1,0:T(2,128)(2,1)} %get-tuple-element.120) | data formatting | bytes 1048576 | tf_op jit(solution)/shard_map/reshape | solution.py:152
  67.1 3.5 %all-to-all-start.3 = ((bf16[4,64,1,1024]{3,1,2,0:T(8,128)(2,1)}), bf16[4,64,1,1024]{3,1,2,0:T(8,128)(2,1)S(1)}, u32[]{:S(2)}, u32[]{:S(2)}) async-start(bf16[4,64,1,1024]{3,1,2,0:T(8,128)(2,1)} %bitcast.22), calls=%async_computation.3 | async-start | bytes 1048576 | tf_op jit(solution)/shard_map/all_to_all | solution.py:153
  70.6 0.7 sort.48
  71.4 1.3 %gather_fusion.2 = bf16[4,4,64,128]{3,2,1,0:T(8,128)(2,1)} fusion(bf16[4,4,64,128]{3,2,1,0:T(8,128)(2,1)S(1)} %get-tuple-element.190, s32[1024]{0:T(1024)S(1)} %pad_clamp_fusion), kind=kCustom, calls=%fused_computation.2 | custom fusion | bytes 524304 | tf_op jit(solution)/shard_map/gather | solution.py:106
  72.7 1.3 %gather_fusion.1 = bf16[4,4,64,128]{3,2,1,0:T(8,128)(2,1)} fusion(bf16[4,4,64,128]{3,2,1,0:T(8,128)(2,1)S(1)} %get-tuple-element.191, s32[1024]{0:T(1024)S(1)} %pad_clamp_fusion), kind=kCustom, calls=%fused_computation.1 | custom fusion | bytes 524304 | tf_op jit(solution)/shard_map/gather | solution.py:105
  73.9 12.0 %all-to-all-done.3 = bf16[4,64,1,1024]{3,1,2,0:T(8,128)(2,1)S(1)} async-done(((bf16[4,64,1,1024]{3,1,2,0:T(8,128)(2,1)}), bf16[4,64,1,1024]{3,1,2,0:T(8,128)(2,1)S(1)}, u32[]{:S(2)}, u32[]{:S(2)}) %all-to-all-start.3) | async-done | bytes 524320 | tf_op jit(solution)/shard_map/all_to_all | solution.py:153
  85.9 0.4 copy.78
  86.3 1.2 %reshape.239 = bf16[1,64,4096]{2,1,0:T(8,128)(2,1)} reshape(bf16[1,64,4,1,1024]{4,2,1,3,0:T(4,128)(2,1)S(1)} %copy.78) | data formatting | bytes 1048576 | tf_op jit(solution)/shard_map/reshape | solution.py:154
  (50 shorter events, 1.2 us)
Async XLA Ops:
  0.6 8.4 %copy-start.5 = (s32[2,4]{1,0:T(2,128)S(1)}, s32[2,4]{1,0:T(2,128)}, u32[]{:S(2)}) copy-start(s32[2,4]{1,0:T(2,128)} %param.10) | copy-start | bytes 100
  0.6 8.7 %copy-start.4 = (s32[2,8]{1,0:T(2,128)S(1)}, s32[2,8]{1,0:T(2,128)}, u32[]{:S(2)}) copy-start(s32[2,8]{1,0:T(2,128)} %param.11) | copy-start | bytes 196
  0.7 9.7 %copy-start.3 = (bf16[1,64,2048]{2,1,0:T(8,128)(2,1)S(1)}, bf16[1,64,2048]{2,1,0:T(8,128)(2,1)}, u32[]{:S(2)}) copy-start(bf16[1,64,2048]{2,1,0:T(8,128)(2,1)} %param.9) | copy-start | bytes 786436
  2.6 18.8 %copy-start = (bf16[1,64,4096]{2,1,0:T(8,128)(2,1)S(1)}, bf16[1,64,4096]{2,1,0:T(8,128)(2,1)}, u32[]{:S(2)}) copy-start(bf16[1,64,4096]{2,1,0:T(8,128)(2,1)} %param.7) | copy-start | bytes 1572868
  2.6 15.4 %all-to-all-start = ((bf16[64,4,512]{2,0,1:T(8,128)(2,1)}), bf16[64,4,512]{2,0,1:T(8,128)(2,1)S(1)}, u32[]{:S(2)}, u32[]{:S(2)}) async-start(bf16[64,4,512]{2,0,1:T(8,128)(2,1)} %copy.70), calls=%async_computation | async-start | bytes 524288 | tf_op jit(solution)/shard_map/all_to_all | solution.py:69
  18.0 10.4 %all-to-all-start.1 = ((bf16[64,4,512]{2,0,1:T(8,128)(2,1)}), bf16[64,4,512]{2,0,1:T(8,128)(2,1)S(1)}, u32[]{:S(2)}, u32[]{:S(2)}) async-start(bf16[64,4,512]{2,0,1:T(8,128)(2,1)} %copy.71), calls=%async_computation.1 | async-start | bytes 524288 | tf_op jit(solution)/shard_map/all_to_all | solution.py:70
  28.4 15.2 %all-to-all-start.2 = ((bf16[64,4,1024]{2,0,1:T(8,128)(2,1)}), bf16[64,4,1024]{2,0,1:T(8,128)(2,1)S(1)}, u32[]{:S(2)}, u32[]{:S(2)}) async-start(bf16[64,4,1024]{2,0,1:T(8,128)(2,1)} %copy.72), calls=%async_computation.2 | async-start | bytes 1048576 | tf_op jit(solution)/shard_map/all_to_all | solution.py:68
  33.3 15.0 %collective-permute-start = (bf16[2,256,512]{2,1,0:T(8,128)(2,1)S(1)}, bf16[2,256,512]{2,1,0:T(8,128)(2,1)}, u32[]{:S(2)}, u32[]{:S(2)}) collective-permute-start(bf16[2,256,512]{2,1,0:T(8,128)(2,1)S(1)} %pad_maximum_fusion), channel_id=1, source_target_pairs={{0,2},{1,3},{4,6},{5,7},{8,10},{9,11},{12,14},{13,15},{16,18},{17,... | collective-permute-start | bytes 1572872 | tf_op jit(solution)/shard_map/ppermute | solution.py:20
  43.6 23.5 %all-to-all-start.4 = ((bf16[2,4,1,4,64,128]{5,4,3,0,2,1:T(8,128)(2,1)}), bf16[2,4,1,4,64,128]{5,4,3,0,2,1:T(8,128)(2,1)S(1)}, u32[]{:S(2)}, u32[]{:S(2)}) async-start(bf16[2,4,1,4,64,128]{5,4,3,0,2,1:T(8,128)(2,1)} %bitcast.30), calls=%async_computation.4 | async-start | bytes 1048576 | tf_op jit(solution)/shard_map/all_to_all | solution.py:93
  55.1 1.0 %copy-start.1 = (bf16[2,128,4,2,128]{4,3,2,1,0:T(2,128)(2,1)S(1)}, bf16[2,128,4,2,128]{4,3,2,1,0:T(2,128)(2,1)}, u32[]{:S(2)}) copy-start(bf16[2,128,4,2,128]{4,3,2,1,0:T(2,128)(2,1)} %get-tuple-element.278) | copy-start | bytes 1572868 | tf_op jit(solution)/shard_map/while
  56.4 0.8 copy-start.2
  62.8 1.0 %copy-start.1 = (bf16[2,128,4,2,128]{4,3,2,1,0:T(2,128)(2,1)S(1)}, bf16[2,128,4,2,128]{4,3,2,1,0:T(2,128)(2,1)}, u32[]{:S(2)}) copy-start(bf16[2,128,4,2,128]{4,3,2,1,0:T(2,128)(2,1)} %get-tuple-element.278) | copy-start | bytes 1572868 | tf_op jit(solution)/shard_map/while
  64.1 0.8 copy-start.2
  67.1 18.8 %all-to-all-start.3 = ((bf16[4,64,1,1024]{3,1,2,0:T(8,128)(2,1)}), bf16[4,64,1,1024]{3,1,2,0:T(8,128)(2,1)S(1)}, u32[]{:S(2)}, u32[]{:S(2)}) async-start(bf16[4,64,1,1024]{3,1,2,0:T(8,128)(2,1)} %bitcast.22), calls=%async_computation.3 | async-start | bytes 1048576 | tf_op jit(solution)/shard_map/all_to_all | solution.py:153
where the time goes:
time: 88.3 us; the launch traced here: 87.5 us
  waiting for transfers between devices  27.5 us (31%)
  starting transfers between devices  24.5 us (28%)
  local copies, waits for them, and re-layouts  19.2 us (22%)
  loops' own time  6.61 us (7%)
  other arithmetic  6.52 us (7%)
  matrix products  2.22 us (3%)
  between operations  0.94 us (1%)
    all_to_all x1, waiting for transfers between devices, body(): lax.all_to_all(outgoing_heads, 'ulysses', split_axis=0, concat_axis=2, ti...  12 us
    another operation x1, loops' own time, body(): blocks = lax.map(attend, starts)  6.61 us
    all_to_all x1, waiting for transfers between devices, body(): lax.all_to_all(key_split, 'ulysses', split_axis=1, concat_axis=0, tiled=T...  6.59 us
    all_to_all x1, starting transfers between devices, body(): lax.all_to_all(key_split, 'ulysses', split_axis=1, concat_axis=0, tiled=T...  6.48 us
    all_to_all x1, waiting for transfers between devices, body(): lax.all_to_all(query_split, 'ulysses', split_axis=1, concat_axis=0, tiled...  4.61 us
    all_to_all x1, waiting for transfers between devices, body(): lax.all_to_all(value_split, 'ulysses', split_axis=1, concat_axis=0, tiled...  4.36 us
    ppermute x1, starting transfers between devices, from_behind(): return lax.ppermute(block, axis, route)  4.21 us
    all_to_all x1, starting transfers between devices, body(): lax.all_to_all(outgoing_heads, 'ulysses', split_axis=0, concat_axis=2, ti...  3.47 us
  transfers between devices with their start and end apart: 6, of which 4 were waited for; matrix products, arithmetic and copies ran while one was open for 25% of the time, Pallas kernels for 0%

commit v1 on v0

--- a/solution.py
+++ b/solution.py
@@ -12,6 +12,18 @@
 QUERY_SCALE = 144.0 ** (-0.5)
 SOFT_CAP = 50.0
 ROPE_BASE = 10000.0
+
+
+def exchange_directly(array, axis, split, join):
+    ways, here = (lax.axis_size(axis), lax.axis_index(axis))
+    width = array.shape[split] // ways
+    turned = jnp.roll(array, -here * width, axis=split)
+    got = [lax.slice_in_dim(turned, 0, width, axis=split)]
+    for far in range(1, ways):
+        sent = lax.slice_in_dim(turned, far * width, (far + 1) * width, axis=split)
+        got.append(lax.ppermute(sent, axis, [(d, (d + far) % ways) for d in range(ways)]))
+    line = jnp.concatenate(got[::-1], axis=join)
+    return jnp.roll(line, (here + 1) * got[0].shape[join], axis=join)
 
 
 def from_behind(block, axis, distance):
@@ -66,7 +78,7 @@
     query_owner, offsets = request_marks(pages_row, positions)
     queries_moved, keys_moved, values_moved = (
         lax.all_to_all(query_split, "ulysses", split_axis=1, concat_axis=0, tiled=True),
-        lax.all_to_all(key_split, "ulysses", split_axis=1, concat_axis=0, tiled=True),
+        exchange_directly(key_split, "ulysses", 1, 0),
         lax.all_to_all(value_split, "ulysses", split_axis=1, concat_axis=0, tiled=True),
     )
     key_turned = rotate(keys_moved.reshape(shard_rows, kv_local, HD), offsets)

time: 88.3 us -> 92.2 us (1.044)
  starting transfers between devices: 24.5 us -> 27.9 us
  local copies, waits for them, and re-layouts: 19.2 us -> 20.6 us
  waiting for transfers between devices: 27.5 us -> 26.1 us
    ppermute x0 -> x3, waiting for transfers between devices: none -> 7.21 us  [exchange_directly(): lax.ppermute(sent, axis, [(d, (d + far) % ways) for d in range(ways)])]
    all_to_all x1 -> x0, waiting for transfers between devices: 6.59 us -> none  [body(): lax.all_to_all(key_split, 'ulysses', split_axis=1, concat_axis=0, tiled=T...]
    all_to_all x1 -> x0, starting transfers between devices: 6.48 us -> none  [body(): lax.all_to_all(key_split, 'ulysses', split_axis=1, concat_axis=0, tiled=T...]
    ppermute x0 -> x3, starting transfers between devices: none -> 5.9 us  [exchange_directly(): lax.ppermute(sent, axis, [(d, (d + far) % ways) for d in range(ways)])]
    all_to_all x1, waiting for transfers between devices: 4.36 us -> 0.01 us  [body(): lax.all_to_all(value_split, 'ulysses', split_axis=1, concat_axis=0, tiled...]
    all_to_all x1, waiting for transfers between devices: 4.61 us -> 7.59 us  [body(): lax.all_to_all(query_split, 'ulysses', split_axis=1, concat_axis=0, tiled...]
    all_to_all x1, starting transfers between devices: 3.41 us -> 6.35 us  [body(): lax.all_to_all(value_split, 'ulysses', split_axis=1, concat_axis=0, tiled...]
    another operation x3 -> x1, local copies, waits for them, and re-layouts: 1.93 us -> 0.01 us  [the longest x2 1.93 us: body(): key_split = keys[0].reshape(local_rows, ulysses_size, kv_local * HD)]
  transfers between devices with their start and end apart: 6 -> 8, of which waited for: 4 -> 4; matrix products, arithmetic and copies ran while one was open for 25% -> 26% of each run, Pallas kernels for 0% -> 0%
where the time goes in v1:
time: 92.2 us; the launch traced here: 91.5 us
  starting transfers between devices  27.9 us (30%)
  waiting for transfers between devices  26.1 us (28%)
  local copies, waits for them, and re-layouts  20.6 us (22%)
  other arithmetic  7.04 us (8%)
  loops' own time  6.61 us (7%)
  matrix products  2.23 us (2%)
  between operations  0.99 us (1%)
    all_to_all x1, waiting for transfers between devices, body(): lax.all_to_all(outgoing_heads, 'ulysses', split_axis=0, concat_axis=2, ti...  11.3 us
    all_to_all x1, waiting for transfers between devices, body(): lax.all_to_all(query_split, 'ulysses', split_axis=1, concat_axis=0, tiled...  7.59 us
    ppermute x3, waiting for transfers between devices, exchange_directly(): lax.ppermute(sent, axis, [(d, (d + far) % ways) for d in range(ways)])  7.21 us
    another operation x1, loops' own time, body(): blocks = lax.map(attend, starts)  6.61 us
    all_to_all x1, starting transfers between devices, body(): lax.all_to_all(value_split, 'ulysses', split_axis=1, concat_axis=0, tiled...  6.35 us
    ppermute x3, starting transfers between devices, exchange_directly(): lax.ppermute(sent, axis, [(d, (d + far) % ways) for d in range(ways)])  5.9 us
    all_to_all x1, starting transfers between devices, body(): lax.all_to_all(query_split, 'ulysses', split_axis=1, concat_axis=0, tiled...  4.52 us
    ppermute x1, starting transfers between devices, from_behind(): return lax.ppermute(block, axis, route)  4.22 us
  transfers between devices with their start and end apart: 8, of which 4 were waited for; matrix products, arithmetic and copies ran while one was open for 26% of the time, Pallas kernels for 0%

profile of v1, /device:TPU:0, one launch (start us, length us, event | category | flops | bytes accessed | tf_op | source)
XLA Modules:
  0.0 91.5 jit_solution(4448681678967332824)
XLA Ops:
  0.6 1.2 %reshape_squeeze.10 = bf16[64,4,512]{2,1,0:T(4,128)(2,1)S(1)} reshape(bf16[1,64,2048]{2,1,0:T(8,128)(2,1)} %param.9) | data formatting | bytes 524288 | tf_op jit(solution)/shard_map/reshape;squeeze | solution.py:75
  1.8 0.7 copy.76
  2.6 6.3 %all-to-all-start = ((bf16[64,4,512]{2,0,1:T(8,128)(2,1)}), bf16[64,4,512]{2,0,1:T(8,128)(2,1)S(1)}, u32[]{:S(2)}, u32[]{:S(2)}) async-start(bf16[64,4,512]{2,0,1:T(8,128)(2,1)} %copy.76), calls=%async_computation | async-start | bytes 524288 | tf_op jit(solution)/shard_map/all_to_all | solution.py:82
  8.9 0.3 copy.75
  9.2 0.3 fusion.9
  9.6 2.1 %collective-permute-start.2 = (bf16[64,1,512]{0,2,1:T(8,128)(2,1)S(1)}, bf16[64,1,512]{0,2,1:T(8,128)(2,1)S(1)}, u32[]{:S(2)}, u32[]{:S(2)}) collective-permute-start(bf16[64,1,512]{0,2,1:T(8,128)(2,1)S(1)} %get-tuple-element.193), channel_id=1, source_target_pairs={{0,4},{4,8},{8,12},{12,0},{1,5},{5,9},{9,13},{13,1},{2,6},{6,10},{... | collective-permute-start | bytes 196616 | tf_op jit(solution)/shard_map/ppermute | solution.py:24
  11.6 2.4 %collective-permute-start.1 = (bf16[64,1,512]{0,2,1:T(8,128)(2,1)S(1)}, bf16[64,1,512]{0,2,1:T(8,128)(2,1)S(1)}, u32[]{:S(2)}, u32[]{:S(2)}) collective-permute-start(bf16[64,1,512]{0,2,1:T(8,128)(2,1)S(1)} %get-tuple-element.194), channel_id=1, source_target_pairs={{0,8},{4,12},{8,0},{12,4},{1,9},{5,13},{9,1},{13,5},{2,10},{6,14},... | collective-permute-start | bytes 196616 | tf_op jit(solution)/shard_map/ppermute | solution.py:24
  14.0 1.5 %collective-permute-start = (bf16[64,1,512]{0,2,1:T(8,128)(2,1)S(1)}, bf16[64,1,512]{0,2,1:T(8,128)(2,1)S(1)}, u32[]{:S(2)}, u32[]{:S(2)}) collective-permute-start(bf16[64,1,512]{0,2,1:T(8,128)(2,1)S(1)} %get-tuple-element.195), channel_id=1, source_target_pairs={{0,12},{4,0},{8,4},{12,8},{1,13},{5,1},{9,5},{13,9},{2,14},{6,2},{... | collective-permute-start | bytes 196616 | tf_op jit(solution)/shard_map/ppermute | solution.py:24
  15.5 0.2 reduce-window.4
  15.9 0.7 sort.46
  16.8 0.3 multiply_cosine_fusion
  17.3 0.1 copy.80
  17.4 0.4 reshape_squeeze.11
  17.8 1.0 %copy.78 = bf16[64,4,1024]{2,0,1:T(8,128)(2,1)} copy(bf16[64,4,1024]{2,1,0:T(4,128)(2,1)S(1)} %reshape_squeeze.11) | data formatting | bytes 1048576 | tf_op jit(solution)/shard_map/reshape;squeeze | solution.py:73
  18.8 0.6 sort.47
  19.5 0.5 iota_multiply_fusion
  20.0 1.5 %collective-permute-done.2 = bf16[64,1,512]{0,2,1:T(8,128)(2,1)S(1)} collective-permute-done((bf16[64,1,512]{0,2,1:T(8,128)(2,1)S(1)}, bf16[64,1,512]{0,2,1:T(8,128)(2,1)S(1)}, u32[]{:S(2)}, u32[]{:S(2)}) %collective-permute-start.2) | collective-permute-done | bytes 65568 | tf_op jit(solution)/shard_map/ppermute | solution.py:24
  21.5 5.7 %collective-permute-done.1 = bf16[64,1,512]{0,2,1:T(8,128)(2,1)S(1)} collective-permute-done((bf16[64,1,512]{0,2,1:T(8,128)(2,1)S(1)}, bf16[64,1,512]{0,2,1:T(8,128)(2,1)S(1)}, u32[]{:S(2)}, u32[]{:S(2)}) %collective-permute-start.1) | collective-permute-done | bytes 65568 | tf_op jit(solution)/shard_map/ppermute | solution.py:24
  27.2 0.5 concatenate.27
  27.7 4.5 %all-to-all-start.1 = ((bf16[64,4,1024]{2,0,1:T(8,128)(2,1)}), bf16[64,4,1024]{2,0,1:T(8,128)(2,1)S(1)}, u32[]{:S(2)}, u32[]{:S(2)}) async-start(bf16[64,4,1024]{2,0,1:T(8,128)(2,1)} %copy.78), calls=%async_computation.1 | async-start | bytes 1048576 | tf_op jit(solution)/shard_map/all_to_all | solution.py:80
  32.3 0.1 constant_dynamic-slice_fusion.3
  32.6 0.2 copy.87
  32.7 0.1 copy.77
  33.1 4.2 %collective-permute-start.3 = (bf16[2,256,512]{2,1,0:T(8,128)(2,1)S(1)}, bf16[2,256,512]{2,1,0:T(8,128)(2,1)}, u32[]{:S(2)}, u32[]{:S(2)}) collective-permute-start(bf16[2,256,512]{2,1,0:T(8,128)(2,1)S(1)} %pad_maximum_fusion), channel_id=1, source_target_pairs={{0,2},{1,3},{4,6},{5,7},{8,10},{9,11},{12,14},{13,15},{16,18},{17,... | collective-permute-start | bytes 1572872 | tf_op jit(solution)/shard_map/ppermute | solution.py:32
  37.3 1.4 %gather_fusion = bf16[4,2,64,4,128]{4,2,3,1,0:T(8,128)(2,1)} fusion(bf16[2,4,64,4,128]{4,2,3,1,0:T(8,128)(2,1)S(1)} %pad_maximum_fusion.2, s32[1024]{0:T(1024)S(1)} %pad_clamp_fusion.1), kind=kCustom, calls=%fused_computation | custom fusion | bytes 1048592 | tf_op jit(solution)/shard_map/gather | solution.py:102
  38.7 7.6 %all-to-all-done.1 = bf16[64,4,1024]{2,0,1:T(8,128)(2,1)S(1)} async-done(((bf16[64,4,1024]{2,0,1:T(8,128)(2,1)}), bf16[64,4,1024]{2,0,1:T(8,128)(2,1)S(1)}, u32[]{:S(2)}, u32[]{:S(2)}) %all-to-all-start.1) | async-done | bytes 524320 | tf_op jit(solution)/shard_map/all_to_all | solution.py:80
  46.3 3.5 %all-to-all-start.3 = ((bf16[2,4,1,4,64,128]{5,4,3,0,2,1:T(8,128)(2,1)}), bf16[2,4,1,4,64,128]{5,4,3,0,2,1:T(8,128)(2,1)S(1)}, u32[]{:S(2)}, u32[]{:S(2)}) async-start(bf16[2,4,1,4,64,128]{5,4,3,0,2,1:T(8,128)(2,1)} %bitcast.32), calls=%async_computation.3 | async-start | bytes 1048576 | tf_op jit(solution)/shard_map/all_to_all | solution.py:105
  49.8 0.1 bitcast_convert_fusion
  49.9 0.2 copy.110
  50.1 0.5 subtract_convert_fusion
  50.8 0.3 pad_maximum_fusion.1
  51.1 1.1 %maximum_maximum_fusion = bf16[2,512,512]{2,1,0:T(8,128)(2,1)S(1)} fusion(bf16[1,256,512]{2,1,0:T(8,128)(2,1)S(1)} %bitcast.109, bf16[1,256,512]{2,1,0:T(8,128)(2,1)S(1)} %copy.77, bf16[2,256,512]{2,1,0:T(8,128)(2,1)} %collective-permute-done.3), kind=kLoop, calls=%fused_computation.22 | loop fusion | flops 3145728 | bytes 2097152 | tf_op jit(solution)/shard_map/concatenate | solution.py:123
  52.2 16.6 %while.12 = (s32[]{:T(128)}, bf16[2,128,4,2,128]{4,3,2,1,0:T(2,128)(2,1)}, s32[2]{0:T(128)}, bf16[2,512,512]{2,1,0:T(8,128)(2,1)S(1)}, s32[256]{0:T(256)S(1)}, /...) while((s32[]{:T(128)}, ...), condition=%wide.region_6.7_spmd, body=%wide.region_4.6_spmd.sunk | while | flops 203898240 | bytes 11392056 | solution.py:163
  52.2 1.2 %dynamic_slice.95 = s32[1]{0:T(128)} dynamic-slice(s32[2]{0:T(128)} %get-tuple-element.297, s32[]{:T(128)S(6)} %copy.122), dynamic_slice_sizes={1} | dynamic-slice | bytes 12 | tf_op jit(solution)/shard_map/while/body/jit(dynamic_index_in_dim)/dynamic_slice | solution.py:163
  57.0 0.1 fusion.31
  57.1 0.2 constant_dynamic-slice_fusion.5
  57.3 0.2 copy.116
  57.6 0.2 copy.117
  57.8 0.7 fusion.32
  58.5 0.4 fusion.33
  58.9 0.2 copy.118
  59.1 0.5 copy-done.1
  59.6 0.2 constant_dynamic-update-slice_fusion.2
  59.8 0.8 copy-done.2
  60.6 1.2 %dynamic_slice.95 = s32[1]{0:T(128)} dynamic-slice(s32[2]{0:T(128)} %get-tuple-element.297, s32[]{:T(128)S(6)} %copy.122), dynamic_slice_sizes={1} | dynamic-slice | bytes 12 | tf_op jit(solution)/shard_map/while/body/jit(dynamic_index_in_dim)/dynamic_slice | solution.py:163
  65.3 0.1 fusion.31
  65.5 0.2 constant_dynamic-slice_fusion.5
  65.7 0.2 copy.116
  65.9 0.2 copy.117
  66.1 0.7 fusion.32
  66.8 0.4 fusion.33
  67.2 0.2 copy.118
  67.4 0.5 copy-done.1
  67.9 0.2 constant_dynamic-update-slice_fusion.2
  68.1 0.8 copy-done.2
  68.9 2.2 %reshape.235 = bf16[4,64,1,1024]{3,1,0,2:T(8,128)(2,1)} reshape(bf16[2,128,4,2,128]{4,3,2,1,0:T(2,128)(2,1)} %get-tuple-element.120) | data formatting | bytes 1048576 | tf_op jit(solution)/shard_map/reshape | solution.py:164
  71.1 3.5 %all-to-all-start.2 = ((bf16[4,64,1,1024]{3,1,2,0:T(8,128)(2,1)}), bf16[4,64,1,1024]{3,1,2,0:T(8,128)(2,1)S(1)}, u32[]{:S(2)}, u32[]{:S(2)}) async-start(bf16[4,64,1,1024]{3,1,2,0:T(8,128)(2,1)} %bitcast.24), calls=%async_computation.2 | async-start | bytes 1048576 | tf_op jit(solution)/shard_map/all_to_all | solution.py:165
  74.6 0.7 subtract_bitcast_fusion
  75.3 0.7 sort.48
  76.1 1.3 %gather_fusion.2 = bf16[4,4,64,128]{3,2,1,0:T(8,128)(2,1)} fusion(bf16[4,4,64,128]{3,2,1,0:T(8,128)(2,1)S(1)} %get-tuple-element.190, s32[1024]{0:T(1024)S(1)} %pad_clamp_fusion), kind=kCustom, calls=%fused_computation.2 | custom fusion | bytes 524304 | tf_op jit(solution)/shard_map/gather | solution.py:118
  77.3 1.3 %gather_fusion.1 = bf16[4,4,64,128]{3,2,1,0:T(8,128)(2,1)} fusion(bf16[4,4,64,128]{3,2,1,0:T(8,128)(2,1)S(1)} %get-tuple-element.191, s32[1024]{0:T(1024)S(1)} %pad_clamp_fusion), kind=kCustom, calls=%fused_computation.1 | custom fusion | bytes 524304 | tf_op jit(solution)/shard_map/gather | solution.py:117
  78.6 11.3 %all-to-all-done.2 = bf16[4,64,1,1024]{3,1,2,0:T(8,128)(2,1)S(1)} async-done(((bf16[4,64,1,1024]{3,1,2,0:T(8,128)(2,1)}), bf16[4,64,1,1024]{3,1,2,0:T(8,128)(2,1)S(1)}, u32[]{:S(2)}, u32[]{:S(2)}) %all-to-all-start.2) | async-done | bytes 524320 | tf_op jit(solution)/shard_map/all_to_all | solution.py:165
  89.9 0.4 copy.86
  90.3 1.2 %reshape.236 = bf16[1,64,4096]{2,1,0:T(8,128)(2,1)} reshape(bf16[1,64,4,1,1024]{4,2,1,3,0:T(4,128)(2,1)S(1)} %copy.86) | data formatting | bytes 1048576 | tf_op jit(solution)/shard_map/reshape | solution.py:166
  (58 shorter events, 1.8 us)
Async XLA Ops:
  0.6 8.3 %copy-start.3 = (bf16[1,64,2048]{2,1,0:T(8,128)(2,1)S(1)}, bf16[1,64,2048]{2,1,0:T(8,128)(2,1)}, u32[]{:S(2)}) copy-start(bf16[1,64,2048]{2,1,0:T(8,128)(2,1)} %param.8) | copy-start | bytes 786436
  2.6 25.2 %all-to-all-start = ((bf16[64,4,512]{2,0,1:T(8,128)(2,1)}), bf16[64,4,512]{2,0,1:T(8,128)(2,1)S(1)}, u32[]{:S(2)}, u32[]{:S(2)}) async-start(bf16[64,4,512]{2,0,1:T(8,128)(2,1)} %copy.76), calls=%async_computation | async-start | bytes 524288 | tf_op jit(solution)/shard_map/all_to_all | solution.py:82
  9.2 6.3 %copy-start.5 = (s32[2,4]{1,0:T(2,128)S(1)}, s32[2,4]{1,0:T(2,128)}, u32[]{:S(2)}) copy-start(s32[2,4]{1,0:T(2,128)} %param.10) | copy-start | bytes 100
  9.2 6.5 %copy-start.4 = (s32[2,8]{1,0:T(2,128)S(1)}, s32[2,8]{1,0:T(2,128)}, u32[]{:S(2)}) copy-start(s32[2,8]{1,0:T(2,128)} %param.11) | copy-start | bytes 196
  9.5 7.9 %copy-start = (bf16[1,64,4096]{2,1,0:T(8,128)(2,1)S(1)}, bf16[1,64,4096]{2,1,0:T(8,128)(2,1)}, u32[]{:S(2)}) copy-start(bf16[1,64,4096]{2,1,0:T(8,128)(2,1)} %param.7) | copy-start | bytes 1572868
  9.6 12.0 %collective-permute-start.2 = (bf16[64,1,512]{0,2,1:T(8,128)(2,1)S(1)}, bf16[64,1,512]{0,2,1:T(8,128)(2,1)S(1)}, u32[]{:S(2)}, u32[]{:S(2)}) collective-permute-start(bf16[64,1,512]{0,2,1:T(8,128)(2,1)S(1)} %get-tuple-element.193), channel_id=1, source_target_pairs={{0,4},{4,8},{8,12},{12,0},{1,5},{5,9},{9,13},{13,1},{2,6},{6,10},{... | collective-permute-start | bytes 196616 | tf_op jit(solution)/shard_map/ppermute | solution.py:24
  11.6 15.6 %collective-permute-start.1 = (bf16[64,1,512]{0,2,1:T(8,128)(2,1)S(1)}, bf16[64,1,512]{0,2,1:T(8,128)(2,1)S(1)}, u32[]{:S(2)}, u32[]{:S(2)}) collective-permute-start(bf16[64,1,512]{0,2,1:T(8,128)(2,1)S(1)} %get-tuple-element.194), channel_id=1, source_target_pairs={{0,8},{4,12},{8,0},{12,4},{1,9},{5,13},{9,1},{13,5},{2,10},{6,14},... | collective-permute-start | bytes 196616 | tf_op jit(solution)/shard_map/ppermute | solution.py:24
  14.0 13.2 %collective-permute-start = (bf16[64,1,512]{0,2,1:T(8,128)(2,1)S(1)}, bf16[64,1,512]{0,2,1:T(8,128)(2,1)S(1)}, u32[]{:S(2)}, u32[]{:S(2)}) collective-permute-start(bf16[64,1,512]{0,2,1:T(8,128)(2,1)S(1)} %get-tuple-element.195), channel_id=1, source_target_pairs={{0,12},{4,0},{8,4},{12,8},{1,13},{5,1},{9,5},{13,9},{2,14},{6,2},{... | collective-permute-start | bytes 196616 | tf_op jit(solution)/shard_map/ppermute | solution.py:24
  27.7 18.6 %all-to-all-start.1 = ((bf16[64,4,1024]{2,0,1:T(8,128)(2,1)}), bf16[64,4,1024]{2,0,1:T(8,128)(2,1)S(1)}, u32[]{:S(2)}, u32[]{:S(2)}) async-start(bf16[64,4,1024]{2,0,1:T(8,128)(2,1)} %copy.78), calls=%async_computation.1 | async-start | bytes 1048576 | tf_op jit(solution)/shard_map/all_to_all | solution.py:80
  33.1 18.0 %collective-permute-start.3 = (bf16[2,256,512]{2,1,0:T(8,128)(2,1)S(1)}, bf16[2,256,512]{2,1,0:T(8,128)(2,1)}, u32[]{:S(2)}, u32[]{:S(2)}) collective-permute-start(bf16[2,256,512]{2,1,0:T(8,128)(2,1)S(1)} %pad_maximum_fusion), channel_id=1, source_target_pairs={{0,2},{1,3},{4,6},{5,7},{8,10},{9,11},{12,14},{13,15},{16,18},{17,... | collective-permute-start | bytes 1572872 | tf_op jit(solution)/shard_map/ppermute | solution.py:32
  46.3 24.8 %all-to-all-start.3 = ((bf16[2,4,1,4,64,128]{5,4,3,0,2,1:T(8,128)(2,1)}), bf16[2,4,1,4,64,128]{5,4,3,0,2,1:T(8,128)(2,1)S(1)}, u32[]{:S(2)}, u32[]{:S(2)}) async-start(bf16[2,4,1,4,64,128]{5,4,3,0,2,1:T(8,128)(2,1)} %bitcast.32), calls=%async_computation.3 | async-start | bytes 1048576 | tf_op jit(solution)/shard_map/all_to_all | solution.py:105
  58.5 1.0 %copy-start.1 = (bf16[2,128,4,2,128]{4,3,2,1,0:T(2,128)(2,1)S(1)}, bf16[2,128,4,2,128]{4,3,2,1,0:T(2,128)(2,1)}, u32[]{:S(2)}) copy-start(bf16[2,128,4,2,128]{4,3,2,1,0:T(2,128)(2,1)} %get-tuple-element.282) | copy-start | bytes 1572868 | tf_op jit(solution)/shard_map/while
  59.8 0.8 copy-start.2
  66.8 1.0 %copy-start.1 = (bf16[2,128,4,2,128]{4,3,2,1,0:T(2,128)(2,1)S(1)}, bf16[2,128,4,2,128]{4,3,2,1,0:T(2,128)(2,1)}, u32[]{:S(2)}) copy-start(bf16[2,128,4,2,128]{4,3,2,1,0:T(2,128)(2,1)} %get-tuple-element.282) | copy-start | bytes 1572868 | tf_op jit(solution)/shard_map/while
  68.1 0.8 copy-start.2
  71.1 18.8 %all-to-all-start.2 = ((bf16[4,64,1,1024]{3,1,2,0:T(8,128)(2,1)}), bf16[4,64,1,1024]{3,1,2,0:T(8,128)(2,1)S(1)}, u32[]{:S(2)}, u32[]{:S(2)}) async-start(bf16[4,64,1,1024]{3,1,2,0:T(8,128)(2,1)} %bitcast.24), calls=%async_computation.2 | async-start | bytes 1048576 | tf_op jit(solution)/shard_map/all_to_all | solution.py:165
